TPU v7x, 32 devices: a whole 2x2x4 slice. The times are simulated.
32 devices in a mesh: slide: 2 (over x), col: 16 (over z, y, core).
Axes of the slice: x: 2, y: 2, z: 4, core: 2. Of those that a mesh axis runs over, the one named last changes fastest.
Arguments:
- patches: bfloat16 [256, 128, 512], P(('slide', 'col')), parts along dimension 0, may hold values from -6 to 6
- tissue: int32 [256, 128], P(('slide', 'col')), parts along dimension 0, may hold values from 0 to 1, as said below
- w_query: bfloat16 [512, 512], replicated, may hold values from -0.25 to 0.25
- w_key: bfloat16 [512, 512], replicated, may hold values from -0.25 to 0.25
- w_value: bfloat16 [512, 512], replicated, may hold values from -0.25 to 0.25
- w_out: bfloat16 [512, 512], replicated, may hold values from -0.25 to 0.25
- agent_tokens: bfloat16 [256, 512], replicated, may hold values from -100 to 100
- kernel_seven: float32 [7, 7, 512], replicated, may hold values from -0.875 to 0.875
- kernel_five: float32 [5, 5, 512], replicated, may hold values from -1.25 to 1.25
- kernel_three: float32 [3, 3, 512], replicated, may hold values from -2 to 2
Outputs:
- mixed: bfloat16 [256, 128, 512], P(('slide', 'col')), parts along dimension 0
There are 2 independent parts, one for each index of `slide`. A program takes and returns all parts, laid end to end along the dimension named above; an argument that names none is the same for every part. Nothing has to cross between parts.
Inputs may be any that keep to these rules, and one draw needn't show every extreme that they name: tissue holds 0 or 1; each slide has at least one tissue patch.
All inputs are finite; a program needn't handle non-finite values.
Results may differ from a plain program's by a relative error of at most 0.007.
The roundings to bfloat16 on the way count: a program that leaves them out, or rounds other values in their place, can miss the bound.
Values may be sent and summed in bfloat16 or wider, within the bound.
A program may use at most 128 MiB of HBM per device.

v0:
```python
import jax
import jax.numpy as jnp
from jax import lax
from jax.sharding import PartitionSpec as P

HEADS = 8


def with_halo(x, sides, width):
    for axis, dim in sides:
        peers, length = (lax.axis_size(axis), x.shape[dim])
        up = [(i, (i + 1) % peers) for i in range(peers - 1)]
        down = [(j, i) for i, j in up]
        last = lax.slice_in_dim(x, length - width, length, axis=dim)
        leading = lax.slice_in_dim(x, 0, width, axis=dim)
        before = lax.ppermute(last, axis, up)
        after = lax.ppermute(leading, axis, down)
        x = jnp.concatenate([before, x, after], axis=dim)
    return x


def joined_kernel(kernel_seven, kernel_five, kernel_three):
    merged = kernel_seven + jnp.pad(kernel_five, ((1, 1), (1, 1), (0, 0)))
    return merged + jnp.pad(kernel_three, ((2, 2), (2, 2), (0, 0)))


def depthwise(extended, kernel, out_rows, grid_width):
    padded = jnp.pad(extended.astype(jnp.float32), ((0, 0), (3, 3), (0, 0)))
    total = jnp.zeros((out_rows, grid_width, kernel.shape[2]), jnp.float32)
    for row_tap in range(7):
        for col_tap in range(7):
            total = (
                total
                + padded[row_tap : row_tap + out_rows, col_tap : col_tap + grid_width]
                * kernel[row_tap, col_tap]
            )
    return total


def rim_terms(rim, kernel, grid_width, lower_side):
    padded = jnp.pad(rim.astype(jnp.float32), ((0, 0), (3, 3), (0, 0)))
    out_list = []
    for out_row in range(3):
        total = jnp.zeros((grid_width, kernel.shape[2]), jnp.float32)
        for rim_row in range(3):
            row_tap = 6 + rim_row - out_row if lower_side else rim_row - out_row
            if 0 <= row_tap <= 6:
                for col_tap in range(7):
                    total = (
                        total
                        + padded[rim_row, col_tap : col_tap + grid_width] * kernel[row_tap, col_tap]
                    )
        out_list.append(total)
    return jnp.stack(out_list)


def on_device(
    patches,
    tissue,
    w_query,
    w_key,
    w_value,
    w_out,
    agent_tokens,
    kernel_seven,
    kernel_five,
    kernel_three,
):
    band_rows, grid_width, model_dim = patches.shape
    head_dim = model_dim // HEADS
    score_scale = head_dim ** (-0.5)
    flat_tokens = patches.reshape(band_rows * grid_width, model_dim)
    queries = jnp.dot(flat_tokens, w_query, preferred_element_type=jnp.float32).astype(jnp.bfloat16)
    keys_all = jnp.dot(flat_tokens, w_key, preferred_element_type=jnp.float32).astype(jnp.bfloat16)
    values_all = jnp.dot(flat_tokens, w_value, preferred_element_type=jnp.float32).astype(
        jnp.bfloat16
    )
    tissue_flat = tissue.reshape(-1) > 0
    kernel = joined_kernel(kernel_seven, kernel_five, kernel_three)
    peak_list = []
    total_list = []
    weighted_list = []
    for head_index in range(HEADS):
        lower = head_index * head_dim
        agent_head = agent_tokens[:, lower : lower + head_dim]
        scores = (
            lax.dot_general(
                agent_head,
                keys_all[:, lower : lower + head_dim],
                (((1,), (1,)), ((), ())),
                preferred_element_type=jnp.float32,
            )
            * score_scale
        )
        peak_head = jnp.max(jnp.where(tissue_flat[None, :], scores, -1e30), axis=1)
        expo = jnp.where(
            tissue_flat[None, :], jnp.exp(scores - peak_head[:, None]), jnp.float32(0.0)
        )
        total_list.append(jnp.sum(expo, axis=1))
        peak_list.append(peak_head)
        weighted_list.append(
            jnp.dot(
                expo.astype(jnp.bfloat16),
                values_all[:, lower : lower + head_dim],
                preferred_element_type=jnp.float32,
            )
        )
    band_peak = jnp.stack(peak_list)
    band_total = jnp.stack(total_list)
    band_weighted = jnp.stack(weighted_list)
    peak = lax.pmax(band_peak, "col")
    factor = jnp.exp(band_peak - peak)
    totals, weighted = lax.psum((band_total * factor, band_weighted * factor[..., None]), "col")
    agent_values = (weighted / totals[..., None]).astype(jnp.bfloat16)
    attended_list = []
    for head_index in range(HEADS):
        lower = head_index * head_dim
        agent_head = agent_tokens[:, lower : lower + head_dim]
        scores = (
            lax.dot_general(
                queries[:, lower : lower + head_dim],
                agent_head,
                (((1,), (1,)), ((), ())),
                preferred_element_type=jnp.float32,
            )
            * score_scale
        )
        top_score = jnp.max(scores, axis=1, keepdims=True)
        expo = jnp.exp(scores - top_score)
        token_weights = (expo / jnp.sum(expo, axis=1, keepdims=True)).astype(jnp.bfloat16)
        attended_list.append(
            jnp.dot(token_weights, agent_values[head_index], preferred_element_type=jnp.float32)
        )
    attended = jnp.concatenate(attended_list, axis=1).reshape(band_rows, grid_width, model_dim)
    value_grid = values_all.reshape(band_rows, grid_width, model_dim)
    blank_rows = jnp.zeros((3, grid_width, model_dim), jnp.bfloat16)
    local_ext = jnp.concatenate([blank_rows, value_grid, blank_rows], axis=0)
    position = depthwise(local_ext, kernel, band_rows, grid_width)
    extended = with_halo(value_grid, (("col", 0),), 3)
    upper_terms = rim_terms(extended[:3], kernel, grid_width, False)
    lower_terms = rim_terms(extended[-3:], kernel, grid_width, True)
    position = position.at[:3].add(upper_terms)
    position = position.at[band_rows - 3 :].add(lower_terms)
    blended = (attended + position).astype(jnp.bfloat16).reshape(band_rows * grid_width, model_dim)
    mixed = jnp.dot(blended, w_out, preferred_element_type=jnp.float32).astype(jnp.bfloat16)
    return mixed.reshape(band_rows, grid_width, model_dim)


def solution(mesh):
    return jax.shard_map(
        on_device,
        mesh=mesh,
        in_specs=(
            P(("slide", "col"), None, None),
            P(("slide", "col"), None),
            P(),
            P(),
            P(),
            P(),
            P(),
            P(),
            P(),
            P(),
        ),
        out_specs=P(("slide", "col"), None, None),
        check_vma=False,
    )
```

profile of v0, /device:TPU:0, one launch (start us, length us, event | category | flops | bytes accessed | tf_op | source)
XLA Modules:
  0.0 210.2 jit_solution(6135621556300776777)
XLA Ops:
  6.5 1.2 copy-done
  7.8 1.8 convolution_convert_fusion.2
  11.5 0.8 convolution_convert_fusion.1
  13.2 1.1 fusion.93
  16.2 1.5 fusion.91
  18.5 35.4 %pmax.7 = f32[8,256]{1,0:T(8,128)S(1)} all-reduce(f32[8,256]{1,0:T(8,128)S(1)} %stack.110), channel_id=1, replica_groups=mesh['slide'=2,'col'=16] {'col'}, use_global_device_ids=true, to_apply=%region_10.11 | all-reduce | flops 2048 | bytes 16384 | tf_op jit(solution)/shard_map/pmax | solution.py:111
  54.0 0.8 broadcast_multiply_fusion
  55.0 0.9 copy.28
  55.9 2.1 collective-permute-start
  58.2 1.3 collective-permute-start.1
  59.5 1.8 convolution_convert_fusion.3
  61.3 1.8 fusion.237
  63.1 1.9 fusion.238
  65.0 1.8 fusion.239
  66.9 2.0 fusion.240
  68.9 1.8 fusion.241
  70.7 0.9 fusion.242
  71.6 1.9 fusion.243
  73.6 1.9 fusion.244
  75.5 1.5 copy.40
  77.0 1.0 pad_add_fusion
  79.9 31.3 %psum.15 = f32[8,256]{1,0:T(8,128)S(1)} all-reduce(f32[8,256]{1,0:T(8,128)S(1)} %get-tuple-element.45), channel_id=1, replica_groups=mesh['slide'=2,'col'=16] {'col'}, use_global_device_ids=true, to_apply=%region_20.21 | all-reduce | flops 2048 | bytes 16384 | tf_op jit(solution)/shard_map/psum | solution.py:113
  111.3 2.1 %fusion.71 = f32[1024]{0:T(1024)} fusion(f32[1024,256]{0,1:T(8,128)} %get-tuple-element.103, f32[1024]{0:T(1024)} %get-tuple-element.102), kind=kLoop, calls=%fused_computation.163 | loop fusion | flops 523264 | bytes 1056768 | tf_op jit(solution)/shard_map/reduce_sum | solution.py:130
  113.5 2.0 fusion.72
  115.5 0.8 fusion.73
  116.2 0.8 fusion.74
  117.0 0.8 fusion.75
  117.7 0.8 fusion.76
  118.6 2.1 maximum_convert_fusion
  120.6 53.5 %fusion.3 = f32[8,128,512]{2,1,0:T(8,128)S(1)} fusion(f32[14,128,512]{2,1,0:T(8,128)} %maximum_convert_fusion, f32[512]{0:T(512)S(1)} %bitcast.145, f32[512]{0:T(512)S(1)} %bitcast.148, f32[512]{0:T(512)} %bitcast.151, f32[512]{0:T(512)} %bitcast.154, f32[512]{0:T(512)} %bitcast.157, f32[512]{0:T(512)} %bitcast.160, f32[512]{0:T(512)} %bitcast.163, ...), kind=kLoop, calls=%fused_computation.4 | loop fusion | flops 50855936 | bytes 20547584 | tf_op jit(solution)/shard_map/add | solution.py:33
  174.2 2.0 fusion.77
  176.2 2.0 fusion.78
  178.1 1.1 divide_convert_fusion.16
  179.3 2.4 %convolution_dynamic-update-slice_fusion.7 = f32[1024,512]{0,1:T(8,128)} fusion(f32[1024,256]{0,1:T(8,128)} %get-tuple-element.103, f32[1024]{0:T(1024)} %fusion.71, f32[1024]{0:T(1024)} %get-tuple-element.102, bf16[8,256,64]{1,2,0:T(8,128)(2,1)S(1)} %divide_convert_fusion.16), kind=kOutput, calls=%fused_computation.114 | convolution fusion | flops 34340864 | bytes 1351680 | tf_op jit(solution)/shard_map/dot_general | solution.py:132
  181.6 1.0 convolution_dynamic-update-slice_fusion.6
  182.9 1.0 convolution_dynamic-update-slice_fusion.5
  184.1 1.0 convolution_dynamic-update-slice_fusion.4
  185.3 1.0 convolution_dynamic-update-slice_fusion.3
  186.6 1.0 convolution_dynamic-update-slice_fusion.2
  187.8 1.0 convolution_dynamic-update-slice_fusion.1
  189.0 1.0 convolution_dynamic-update-slice_fusion
  190.0 2.9 %copy.39 = f32[1024,512]{1,0:T(8,128)} copy(f32[1024,512]{0,1:T(8,128)} %convolution_dynamic-update-slice_fusion) | data formatting | bytes 4194304 | tf_op jit(solution)/shard_map/reshape | solution.py:134
  193.1 1.1 convert_element_type.81
  194.4 1.4 fusion.165
  196.5 1.1 convert_element_type.82
  197.8 0.7 fusion.178
  199.5 1.1 copy-done.1
  201.7 1.7 convolution_convert_fusion
  (175 shorter events, 11.7 us)
Async XLA Ops:
  6.5 3.0 %copy-start.2 = (bf16[256,512]{1,0:T(8,128)(2,1)S(1)}, bf16[256,512]{1,0:T(8,128)(2,1)}, u32[]{:S(2)}) copy-start(bf16[256,512]{1,0:T(8,128)(2,1)} %param.20) | copy-start | bytes 786436
  6.5 171.6 %all-reduce.7.cloned.1.call-start = ((), (), s32[]{:S(2)}) async-start(), calls=%async_computation | async-start | bytes 1048576 | tf_op jit(solution)/shard_map/psum | solution.py:113
  12.3 42.6 %copy-start.14 = (bf16[1024,512]{0,1:T(8,128)(2,1)}, bf16[1024,512]{0,1:T(8,128)(2,1)S(1)}, u32[]{:S(2)}) copy-start(bf16[1024,512]{0,1:T(8,128)(2,1)S(1)} %convolution_convert_fusion.1) | copy-start | bytes 3145732
  55.9 137.2 %collective-permute-start = (bf16[3,128,512]{2,1,0:T(8,128)(2,1)}, bf16[3,128,512]{2,1,0:T(8,128)(2,1)}, u32[]{:S(2)}, u32[]{:S(2)}) collective-permute-start(bf16[3,128,512]{2,1,0:T(8,128)(2,1)} %bitcast.85), channel_id=1, source_target_pairs={{0,1},{1,2},{2,3},{3,4},{4,5},{5,6},{6,7},{7,8},{8,9},{9,10},{10,1... | collective-permute-start | bytes 1179656 | tf_op jit(solution)/shard_map/ppermute | solution.py:16
  58.2 138.3 %collective-permute-start.1 = (bf16[3,128,512]{2,1,0:T(8,128)(2,1)S(1)}, bf16[3,128,512]{2,1,0:T(8,128)(2,1)}, u32[]{:S(2)}, u32[]{:S(2)}) collective-permute-start(bf16[3,128,512]{2,1,0:T(8,128)(2,1)S(1)} %bitcast.144), channel_id=1, source_target_pairs={{1,0},{2,1},{3,2},{4,3},{5,4},{6,5},{7,6},{8,7},{9,8},{10,9},{11,1... | collective-permute-start | bytes 1179656 | tf_op jit(solution)/shard_map/ppermute | solution.py:17
  71.6 46.1 %copy-start.5 = (f32[1024,256]{0,1:T(8,128)}, f32[1024,256]{0,1:T(8,128)S(1)}, u32[]{:S(2)}) copy-start(f32[1024,256]{0,1:T(8,128)S(1)} %get-tuple-element.115) | copy-start | bytes 3145732
  111.3 4.2 %copy-start.11 = (f32[1024,256]{0,1:T(8,128)S(1)}, f32[1024,256]{0,1:T(8,128)}, u32[]{:S(2)}) copy-start(f32[1024,256]{0,1:T(8,128)} %get-tuple-element.109) | copy-start | bytes 3145732
  111.3 4.2 %copy-start.58 = (f32[1024]{0:T(1024)S(1)}, f32[1024]{0:T(1024)}, u32[]{:S(2)}) copy-start(f32[1024]{0:T(1024)} %get-tuple-element.108) | copy-start | bytes 12292
  111.3 4.9 %copy-start.9 = (f32[1024,256]{0,1:T(8,128)S(1)}, f32[1024,256]{0,1:T(8,128)}, u32[]{:S(2)}) copy-start(f32[1024,256]{0,1:T(8,128)} %get-tuple-element.111) | copy-start | bytes 3145732
  111.3 4.9 %copy-start.56 = (f32[1024]{0:T(1024)S(1)}, f32[1024]{0:T(1024)}, u32[]{:S(2)}) copy-start(f32[1024]{0:T(1024)} %get-tuple-element.110) | copy-start | bytes 12292
  111.3 5.7 %copy-start.7 = (f32[1024,256]{0,1:T(8,128)S(1)}, f32[1024,256]{0,1:T(8,128)}, u32[]{:S(2)}) copy-start(f32[1024,256]{0,1:T(8,128)} %get-tuple-element.113) | copy-start | bytes 3145732
  111.3 5.7 %copy-start.54 = (f32[1024]{0:T(1024)S(1)}, f32[1024]{0:T(1024)}, u32[]{:S(2)}) copy-start(f32[1024]{0:T(1024)} %get-tuple-element.112) | copy-start | bytes 12292
  113.5 4.3 %copy-start.52 = (f32[1024]{0:T(1024)S(1)}, f32[1024]{0:T(1024)}, u32[]{:S(2)}) copy-start(f32[1024]{0:T(1024)} %get-tuple-element.114) | copy-start | bytes 12292
  179.2 2.4 %copy-start.13 = (f32[1024,256]{0,1:T(8,128)S(1)}, f32[1024,256]{0,1:T(8,128)}, u32[]{:S(2)}) copy-start(f32[1024,256]{0,1:T(8,128)} %get-tuple-element.107) | copy-start | bytes 3145732
  179.2 2.4 %copy-start.60 = (f32[1024]{0:T(1024)S(1)}, f32[1024]{0:T(1024)}, u32[]{:S(2)}) copy-start(f32[1024]{0:T(1024)} %get-tuple-element.106) | copy-start | bytes 12292
  193.0 2.8 %copy-start.29 = (f32[1,1,512]{2,1,0:T(1,128)S(1)}, f32[1,1,512]{2,1,0:T(1,128)}, u32[]{:S(2)}) copy-start(f32[1,1,512]{2,1,0:T(1,128)} %get-tuple-element.53) | copy-start | bytes 6148
  193.0 2.9 %copy-start.30 = (f32[1,1,512]{2,1,0:T(1,128)S(1)}, f32[1,1,512]{2,1,0:T(1,128)}, u32[]{:S(2)}) copy-start(f32[1,1,512]{2,1,0:T(1,128)} %get-tuple-element.72) | copy-start | bytes 6148
  193.0 2.9 %copy-start.31 = (f32[1,1,512]{2,1,0:T(1,128)S(1)}, f32[1,1,512]{2,1,0:T(1,128)}, u32[]{:S(2)}) copy-start(f32[1,1,512]{2,1,0:T(1,128)} %get-tuple-element.90) | copy-start | bytes 6148
  193.0 2.9 %copy-start.32 = (f32[1,1,512]{2,1,0:T(1,128)S(1)}, f32[1,1,512]{2,1,0:T(1,128)}, u32[]{:S(2)}) copy-start(f32[1,1,512]{2,1,0:T(1,128)} %get-tuple-element.91) | copy-start | bytes 6148
  193.0 2.9 %copy-start.33 = (f32[1,1,512]{2,1,0:T(1,128)S(1)}, f32[1,1,512]{2,1,0:T(1,128)}, u32[]{:S(2)}) copy-start(f32[1,1,512]{2,1,0:T(1,128)} %get-tuple-element.92) | copy-start | bytes 6148
  193.0 2.9 %copy-start.34 = (f32[1,1,512]{2,1,0:T(1,128)S(1)}, f32[1,1,512]{2,1,0:T(1,128)}, u32[]{:S(2)}) copy-start(f32[1,1,512]{2,1,0:T(1,128)} %get-tuple-element.93) | copy-start | bytes 6148
  193.0 2.9 %copy-start.35 = (f32[1,1,512]{2,1,0:T(1,128)S(1)}, f32[1,1,512]{2,1,0:T(1,128)}, u32[]{:S(2)}) copy-start(f32[1,1,512]{2,1,0:T(1,128)} %get-tuple-element.94) | copy-start | bytes 6148
  193.0 2.9 %copy-start.36 = (f32[1,1,512]{2,1,0:T(1,128)S(1)}, f32[1,1,512]{2,1,0:T(1,128)}, u32[]{:S(2)}) copy-start(f32[1,1,512]{2,1,0:T(1,128)} %get-tuple-element.95) | copy-start | bytes 6148
  193.0 2.9 %copy-start.37 = (f32[1,1,512]{2,1,0:T(1,128)S(1)}, f32[1,1,512]{2,1,0:T(1,128)}, u32[]{:S(2)}) copy-start(f32[1,1,512]{2,1,0:T(1,128)} %get-tuple-element.96) | copy-start | bytes 6148
  193.0 2.9 %copy-start.38 = (f32[1,1,512]{2,1,0:T(1,128)S(1)}, f32[1,1,512]{2,1,0:T(1,128)}, u32[]{:S(2)}) copy-start(f32[1,1,512]{2,1,0:T(1,128)} %get-tuple-element.97) | copy-start | bytes 6148
  193.1 2.9 %copy-start.39 = (f32[1,1,512]{2,1,0:T(1,128)S(1)}, f32[1,1,512]{2,1,0:T(1,128)}, u32[]{:S(2)}) copy-start(f32[1,1,512]{2,1,0:T(1,128)} %get-tuple-element.98) | copy-start | bytes 6148
  193.1 2.9 %copy-start.40 = (f32[1,1,512]{2,1,0:T(1,128)S(1)}, f32[1,1,512]{2,1,0:T(1,128)}, u32[]{:S(2)}) copy-start(f32[1,1,512]{2,1,0:T(1,128)} %get-tuple-element.99) | copy-start | bytes 6148
  193.1 2.9 %copy-start.41 = (f32[1,1,512]{2,1,0:T(1,128)S(1)}, f32[1,1,512]{2,1,0:T(1,128)}, u32[]{:S(2)}) copy-start(f32[1,1,512]{2,1,0:T(1,128)} %get-tuple-element.100) | copy-start | bytes 6148
  193.1 2.9 %copy-start.42 = (f32[1,1,512]{2,1,0:T(1,128)S(1)}, f32[1,1,512]{2,1,0:T(1,128)}, u32[]{:S(2)}) copy-start(f32[1,1,512]{2,1,0:T(1,128)} %get-tuple-element.101) | copy-start | bytes 6148
  194.2 3.4 %copy-start.17 = (f32[1,1,512]{2,1,0:T(1,128)S(1)}, f32[1,1,512]{2,1,0:T(1,128)}, u32[]{:S(2)}) copy-start(f32[1,1,512]{2,1,0:T(1,128)} %get-tuple-element.56) | copy-start | bytes 6148
  194.2 3.4 %copy-start.18 = (f32[1,1,512]{2,1,0:T(1,128)S(1)}, f32[1,1,512]{2,1,0:T(1,128)}, u32[]{:S(2)}) copy-start(f32[1,1,512]{2,1,0:T(1,128)} %get-tuple-element.57) | copy-start | bytes 6148
  194.2 3.4 %copy-start.19 = (f32[1,1,512]{2,1,0:T(1,128)S(1)}, f32[1,1,512]{2,1,0:T(1,128)}, u32[]{:S(2)}) copy-start(f32[1,1,512]{2,1,0:T(1,128)} %get-tuple-element.58) | copy-start | bytes 6148
  194.2 3.4 %copy-start.20 = (f32[1,1,512]{2,1,0:T(1,128)S(1)}, f32[1,1,512]{2,1,0:T(1,128)}, u32[]{:S(2)}) copy-start(f32[1,1,512]{2,1,0:T(1,128)} %get-tuple-element.59) | copy-start | bytes 6148
  194.2 3.4 %copy-start.21 = (f32[1,1,512]{2,1,0:T(1,128)S(1)}, f32[1,1,512]{2,1,0:T(1,128)}, u32[]{:S(2)}) copy-start(f32[1,1,512]{2,1,0:T(1,128)} %get-tuple-element.60) | copy-start | bytes 6148
  194.2 3.4 %copy-start.22 = (f32[1,1,512]{2,1,0:T(1,128)S(1)}, f32[1,1,512]{2,1,0:T(1,128)}, u32[]{:S(2)}) copy-start(f32[1,1,512]{2,1,0:T(1,128)} %get-tuple-element.61) | copy-start | bytes 6148
  194.2 3.4 %copy-start.23 = (f32[1,1,512]{2,1,0:T(1,128)S(1)}, f32[1,1,512]{2,1,0:T(1,128)}, u32[]{:S(2)}) copy-start(f32[1,1,512]{2,1,0:T(1,128)} %get-tuple-element.62) | copy-start | bytes 6148
  194.3 3.4 %copy-start.24 = (f32[1,1,512]{2,1,0:T(1,128)S(1)}, f32[1,1,512]{2,1,0:T(1,128)}, u32[]{:S(2)}) copy-start(f32[1,1,512]{2,1,0:T(1,128)} %get-tuple-element.63) | copy-start | bytes 6148
  194.3 3.4 %copy-start.25 = (f32[1,1,512]{2,1,0:T(1,128)S(1)}, f32[1,1,512]{2,1,0:T(1,128)}, u32[]{:S(2)}) copy-start(f32[1,1,512]{2,1,0:T(1,128)} %get-tuple-element.64) | copy-start | bytes 6148
  194.3 3.4 %copy-start.26 = (f32[1,1,512]{2,1,0:T(1,128)S(1)}, f32[1,1,512]{2,1,0:T(1,128)}, u32[]{:S(2)}) copy-start(f32[1,1,512]{2,1,0:T(1,128)} %get-tuple-element.65) | copy-start | bytes 6148
  194.3 3.4 %copy-start.27 = (f32[1,1,512]{2,1,0:T(1,128)S(1)}, f32[1,1,512]{2,1,0:T(1,128)}, u32[]{:S(2)}) copy-start(f32[1,1,512]{2,1,0:T(1,128)} %get-tuple-element.66) | copy-start | bytes 6148
  194.3 3.4 %copy-start.28 = (f32[1,1,512]{2,1,0:T(1,128)S(1)}, f32[1,1,512]{2,1,0:T(1,128)}, u32[]{:S(2)}) copy-start(f32[1,1,512]{2,1,0:T(1,128)} %get-tuple-element.67) | copy-start | bytes 6148
  194.3 3.4 %copy-start.43 = (f32[1,1,512]{2,1,0:T(1,128)S(1)}, f32[1,1,512]{2,1,0:T(1,128)}, u32[]{:S(2)}) copy-start(f32[1,1,512]{2,1,0:T(1,128)} %get-tuple-element.68) | copy-start | bytes 6148
  194.3 3.4 %copy-start.44 = (f32[1,1,512]{2,1,0:T(1,128)S(1)}, f32[1,1,512]{2,1,0:T(1,128)}, u32[]{:S(2)}) copy-start(f32[1,1,512]{2,1,0:T(1,128)} %get-tuple-element.69) | copy-start | bytes 6148
  194.3 3.4 %copy-start.45 = (f32[1,1,512]{2,1,0:T(1,128)S(1)}, f32[1,1,512]{2,1,0:T(1,128)}, u32[]{:S(2)}) copy-start(f32[1,1,512]{2,1,0:T(1,128)} %get-tuple-element.70) | copy-start | bytes 6148
  194.3 3.4 %copy-start.46 = (f32[1,1,512]{2,1,0:T(1,128)S(1)}, f32[1,1,512]{2,1,0:T(1,128)}, u32[]{:S(2)}) copy-start(f32[1,1,512]{2,1,0:T(1,128)} %get-tuple-element.71) | copy-start | bytes 6148
  194.3 3.4 %copy-start.47 = (f32[1,1,512]{2,1,0:T(1,128)S(1)}, f32[1,1,512]{2,1,0:T(1,128)}, u32[]{:S(2)}) copy-start(f32[1,1,512]{2,1,0:T(1,128)} %get-tuple-element.73) | copy-start | bytes 6148
  194.4 3.4 %copy-start.48 = (f32[1,1,512]{2,1,0:T(1,128)S(1)}, f32[1,1,512]{2,1,0:T(1,128)}, u32[]{:S(2)}) copy-start(f32[1,1,512]{2,1,0:T(1,128)} %get-tuple-element.74) | copy-start | bytes 6148
  194.4 3.4 %copy-start.49 = (f32[1,1,512]{2,1,0:T(1,128)S(1)}, f32[1,1,512]{2,1,0:T(1,128)}, u32[]{:S(2)}) copy-start(f32[1,1,512]{2,1,0:T(1,128)} %get-tuple-element.75) | copy-start | bytes 6148
  (26 other events, 34.4 us)
Sparse Core Ops, SparseCore 0:
  55.0 87.2 all-reduce.6
where the time goes:
time: 211 us; the launch traced here: 210 us
  other arithmetic  77.5 us (37%)
  blocking collectives  66.8 us (32%)
  matrix products  36.2 us (17%)
  between operations  14.4 us (7%)
  local copies, waits for them, and re-layouts  12 us (6%)
  starting transfers between devices  3.36 us (2%)
    add x1, other arithmetic, depthwise(): total + padded[row_tap:row_tap + out_rows, col_tap:col_tap + grid_width]...  53.5 us
    pmax x1, blocking collectives, on_device(): peak = lax.pmax(band_peak, 'col')  35.4 us
    psum x1, blocking collectives, on_device(): lax.psum((band_total * factor, band_weighted * factor[..., None]), 'col')  31.3 us
    dot_general x8, matrix products, on_device(): lax.dot_general(queries[:, lower:lower + head_dim], agent_head, (((1,), (...  14.2 us
    reduce_sum x8, other arithmetic, on_device(): jnp.sum(expo, axis=1, keepdims=True)  11.1 us
    dot_general x8, matrix products, on_device(): jnp.dot(token_weights, agent_values[head_index], preferred_element_type=j...  9.51 us
    unnamed x142, local copies, waits for them, and re-layouts  4.33 us
  transfers between devices with their start and end apart: 3, of which 0 were waited for; matrix products, arithmetic and copies ran while one was open for 50% of the time, Pallas kernels for 0%

commit v1 on v0

v1 whole, which is shorter than its diff:
```python
import functools

import jax
import jax.numpy as jnp
from jax import lax
from jax.experimental import pallas as pl
from jax.experimental.pallas import tpu as pltpu
from jax.sharding import PartitionSpec as P

HEADS = 8
LANES = 128
NONE = -1e30
F32, BF16 = jnp.float32, jnp.bfloat16
NT = (((1,), (1,)), ((), ()))
VMEM = pl.BlockSpec(memory_space=pltpu.VMEM)
LIMIT = 56 * 1024 * 1024


def low_half(shape):
    return lax.broadcasted_iota(jnp.int32, shape, len(shape) - 1) < LANES // 2


def head_agents(ag_ref, head):
    start = head // 2 * LANES
    pair = ag_ref[:, start : start + LANES].astype(F32) * 0.125
    keep = low_half(pair.shape)
    keep = keep if head % 2 == 0 else jnp.logical_not(keep)
    return jnp.where(keep, pair, 0.0).astype(BF16)


def stats_kernel(x_ref, tissue_ref, wk_ref, wv_ref, ag_ref, v_ref, st_ref, k_ref):
    tokens, dim = x_ref.shape
    chunk = 256
    for c in range(0, tokens, chunk):
        x = x_ref[c : c + chunk, :]
        k_ref[c : c + chunk, :] = jnp.dot(x, wk_ref[...], preferred_element_type=F32).astype(BF16)
        v_ref[c : c + chunk, :] = jnp.dot(x, wv_ref[...], preferred_element_type=F32).astype(BF16)
    rows = tissue_ref.shape[0]
    tissue = jnp.concatenate([tissue_ref[r : r + 1, :] for r in range(rows)], axis=1) > 0
    agents = ag_ref.shape[0]
    lane = lax.broadcasted_iota(jnp.int32, (agents, LANES), 1)
    side = jnp.zeros((agents, LANES), F32)
    for pair in range(HEADS // 2):
        start = pair * LANES
        got = []
        for head in (2 * pair, 2 * pair + 1):
            s = lax.dot_general(
                head_agents(ag_ref, head), k_ref[:, start : start + LANES], NT, preferred_element_type=F32
            )
            s = jnp.where(tissue, s, NONE)
            top = jnp.max(s, axis=1, keepdims=True)
            e = jnp.exp(s - jnp.maximum(top, 0.1 * NONE))
            total = jnp.sum(e, axis=1, keepdims=True)
            got.append(
                jnp.dot(e.astype(BF16), v_ref[:, start : start + LANES], preferred_element_type=F32)
            )
            side = jnp.where(lane == head, top, side)
            side = jnp.where(lane == HEADS + head, total, side)
        st_ref[:, start : start + LANES] = jnp.where(lane < LANES // 2, got[0], got[1])
    st_ref[:, dim : dim + LANES] = side


def token_side(x_ref, wq_ref, ag_ref, tw_ref):
    tokens = x_ref.shape[0]
    chunk = 256
    for c in range(0, tokens, chunk):
        q = jnp.dot(x_ref[c : c + chunk, :], wq_ref[...], preferred_element_type=F32).astype(BF16)
        for head in range(HEADS):
            start = head // 2 * LANES
            s = lax.dot_general(
                head_agents(ag_ref, head), q[:, start : start + LANES], NT, preferred_element_type=F32
            )
            e = jnp.exp(s - jnp.max(s, axis=0, keepdims=True))
            share = 1.0 / jnp.sum(e, axis=0, keepdims=True)
            tw_ref[head, :, c : c + chunk] = (e * share).astype(BF16)


def spread_taps(k7_ref, k5_ref, k3_ref, taps_ref):
    for block in range(taps_ref.shape[0]):
        at = slice(block * LANES, block * LANES + LANES)
        for p in range(7):
            for q in range(7):
                tap = k7_ref[p, q : q + 1, at]
                if 1 <= p <= 5 and 1 <= q <= 5:
                    tap = tap + k5_ref[p - 1, q - 1 : q, at]
                if 2 <= p <= 4 and 2 <= q <= 4:
                    tap = tap + k3_ref[p - 2, q - 2 : q - 1, at]
                taps_ref[block, p * 7 + q, :, :] = jnp.broadcast_to(tap, (8, LANES))


def fill_own(v_ref, ext_ref):
    blocks, ext_rows, _, _ = ext_ref.shape
    width = v_ref.shape[1]
    for block in range(blocks):
        at = slice(block * LANES, block * LANES + LANES)
        for r in range(ext_rows):
            ext_ref[block, r, 0:8, :] = jnp.zeros((8, LANES), F32)
            ext_ref[block, r, width + 8 : width + 16, :] = jnp.zeros((8, LANES), F32)
        for r in range(ext_rows - 6):
            ext_ref[block, r + 3, 8 : width + 8, :] = v_ref[r, :, at].astype(F32)


def fill_rim(rim_ref, ext_ref, first, there):
    width = rim_ref.shape[1]
    for block in range(ext_ref.shape[0]):
        at = slice(block * LANES, block * LANES + LANES)
        for r in range(3):
            rim = rim_ref[r, :, at].astype(F32)
            ext_ref[block, first + r, 8 : width + 8, :] = jnp.where(there, rim, 0.0)


def convolve(ext_ref, taps_ref, pos_ref):
    blocks, ext_rows, _, _ = ext_ref.shape
    _, rows, width, _ = pos_ref.shape
    step = 16

    def one(i, carry):
        block = i // (width // step)
        c = pl.multiple_of(i % (width // step) * step, step)
        sums = [jnp.zeros((step, LANES), F32) for _ in range(rows)]
        for q in range(7):
            taps = [jnp.concatenate([taps_ref[block, p * 7 + q]] * (step // 8), axis=0) for p in range(7)]
            for r in range(ext_rows):
                x = ext_ref[block, r, pl.ds(c + (5 + q), step), :]
                for out in range(max(r - 6, 0), min(r + 1, rows)):
                    sums[out] = sums[out] + x * taps[r - out]
        for out in range(rows):
            pos_ref[block, out, pl.ds(c, step), :] = sums[out]
        return carry

    lax.fori_loop(0, blocks * (width // step), one, 0)


def finish(av, tw_ref, pos_ref, wo_ref, out_ref):
    av_t = av.T
    blocks, _, width, _ = pos_ref.shape
    chunk = 256
    for c in range(0, out_ref.shape[0], chunk):
        parts = []
        for head in range(HEADS):
            parts.append(
                jnp.dot(
                    av_t[head * 64 : head * 64 + 64, :],
                    tw_ref[head, :, c : c + chunk],
                    preferred_element_type=F32,
                )
            )
        attended = jnp.concatenate(parts, axis=0).T
        position = jnp.concatenate(
            [
                jnp.concatenate([pos_ref[b, r] for b in range(blocks)], axis=1)
                for r in range(c // width, (c + chunk) // width)
            ],
            axis=0,
        )
        blended = (attended + position).astype(BF16)
        out_ref[c : c + chunk, :] = jnp.dot(blended, wo_ref[...], preferred_element_type=F32).astype(BF16)


def combine(got_ref, dim):
    side = got_ref[:, :, dim : dim + LANES]
    factor = jnp.exp(side - jnp.max(side, axis=0, keepdims=True))
    shape = side.shape
    keep = low_half(shape)

    def spread(x, left):
        a = jnp.broadcast_to(x[:, :, left : left + 1], shape)
        b = jnp.broadcast_to(x[:, :, left + 1 : left + 2], shape)
        return jnp.where(keep, a, b)

    parts = []
    for pair in range(HEADS // 2):
        f = spread(factor, 2 * pair)
        total = jnp.sum(f * spread(side, HEADS + 2 * pair), axis=0)
        weighted = jnp.sum(f * got_ref[:, :, pair * LANES : pair * LANES + LANES], axis=0)
        parts.append(weighted / total)
    return jnp.concatenate(parts, axis=1).astype(BF16)


class Exchange:
    def __init__(self, n, v_ref, st_ref, av_ref, above_ref, below_ref, got_ref, sems):
        self.n, self.me = n, lax.axis_index("col")
        self.v, self.st, self.av, self.got = v_ref, st_ref, av_ref, got_ref
        s1, r1, s2, r2, s3, r3 = sems
        me = self.me
        self.to = [lax.rem(me + k, n) for k in range(1, n)]
        self.source = [lax.rem(me + n - k, n) for k in range(1, n)]
        rows = v_ref.shape[0]

        def remote(src, dst, s, r, peer):
            return pltpu.make_async_remote_copy(
                src_ref=src, dst_ref=dst, send_sem=s, recv_sem=r,
                device_id={"col": peer}, device_id_type=pl.DeviceIdType.MESH,
            )

        self.scatter = [
            remote(st_ref.at[p], got_ref.at[me], s1.at[k], r1.at[k], p) for k, p in enumerate(self.to)
        ]
        self.gather = [
            remote(av_ref.at[me], av_ref.at[me], s2.at[k], r2.at[k], p) for k, p in enumerate(self.to)
        ]
        self.down = remote(v_ref.at[pl.ds(rows - 3, 3)], above_ref, s3.at[0], r3.at[0], lax.rem(me + 1, n))
        self.up = remote(v_ref.at[pl.ds(0, 3)], below_ref, s3.at[1], r3.at[1], lax.rem(me + n - 1, n))

    def enter(self):
        barrier = pltpu.get_barrier_semaphore()
        for p in self.to:
            pl.semaphore_signal(
                barrier, inc=1, device_id={"col": p}, device_id_type=pl.DeviceIdType.MESH
            )
        pl.semaphore_wait(barrier, self.n - 1)

    def start(self):
        for copy in self.scatter:
            copy.start()

        @pl.when(self.me < self.n - 1)
        def _():
            self.down.start()

        @pl.when(self.me > 0)
        def _():
            self.up.start()

        self.got[self.me] = self.st[self.me]

    def reduce(self):
        for copy in self.scatter:
            copy.wait()
        self.av[self.me] = combine(self.got, self.v.shape[2])
        for copy in self.gather:
            copy.start()

    def rims(self):
        @pl.when(self.me < self.n - 1)
        def _():
            self.down.wait_send()
            self.up.wait_recv()

        @pl.when(self.me > 0)
        def _():
            self.down.wait_recv()
            self.up.wait_send()

    def end(self):
        for copy in self.gather:
            copy.wait()


def sem_shapes(n):
    dma = pltpu.SemaphoreType.DMA
    return [dma((n - 1,)), dma((n - 1,)), dma((n - 1,)), dma((n - 1,)), dma((2,)), dma((2,))]


def rest_kernel(
    n, x_ref, wq_ref, wo_ref, ag_ref, k7_ref, k5_ref, k3_ref, v_ref, st_ref,
    out_ref, av_ref, above_ref, below_ref, got_ref, tw_ref, taps_ref, ext_ref, pos_ref, *sems
):
    work = Exchange(n, v_ref, st_ref, av_ref, above_ref, below_ref, got_ref, sems)
    above_ref[...] = jnp.zeros(above_ref.shape, BF16)
    below_ref[...] = jnp.zeros(below_ref.shape, BF16)
    work.enter()
    work.start()
    spread_taps(k7_ref, k5_ref, k3_ref, taps_ref)
    fill_own(v_ref, ext_ref)
    token_side(x_ref, wq_ref, ag_ref, tw_ref)
    work.reduce()
    work.rims()
    fill_rim(above_ref, ext_ref, 0, True)
    fill_rim(below_ref, ext_ref, ext_ref.shape[1] - 3, True)
    convolve(ext_ref, taps_ref, pos_ref)
    work.end()
    av = jnp.concatenate([av_ref[i] for i in range(n)], axis=0)
    finish(av, tw_ref, pos_ref, wo_ref, out_ref)


def on_device(n, patches, tissue, w_query, w_key, w_value, w_out, agent_tokens, k7, k5, k3):
    rows, width, dim = patches.shape
    tokens = rows * width
    agents = agent_tokens.shape[0]
    own = agents // n
    x = patches.reshape(tokens, dim)
    values, stats = pl.pallas_call(
        stats_kernel,
        out_shape=(
            jax.ShapeDtypeStruct((tokens, dim), BF16),
            jax.ShapeDtypeStruct((agents, dim + LANES), F32),
        ),
        in_specs=[VMEM] * 5,
        out_specs=(VMEM, VMEM),
        scratch_shapes=[pltpu.VMEM((tokens, dim), BF16)],
        compiler_params=pltpu.CompilerParams(vmem_limit_bytes=LIMIT),
    )(x, tissue, w_key, w_value, agent_tokens)
    values = values.reshape(rows, width, dim)
    stats = stats.reshape(n, own, dim + LANES)
    rim = (3, width, dim)
    blocks = dim // LANES
    work = [
        pltpu.VMEM((HEADS, agents, tokens), BF16),
        pltpu.VMEM((blocks, 49, 8, LANES), F32),
        pltpu.VMEM((blocks, rows + 6, width + 16, LANES), F32),
        pltpu.VMEM((blocks, rows, width, LANES), F32),
    ]
    out = pl.pallas_call(
        functools.partial(rest_kernel, n),
        out_shape=jax.ShapeDtypeStruct((tokens, dim), BF16),
        in_specs=[VMEM] * 9,
        out_specs=VMEM,
        scratch_shapes=[
            pltpu.VMEM((n, own, dim), BF16),
            pltpu.VMEM(rim, BF16),
            pltpu.VMEM(rim, BF16),
            pltpu.VMEM((n, own, dim + LANES), F32),
        ]
        + work
        + sem_shapes(n),
        compiler_params=pltpu.CompilerParams(
            vmem_limit_bytes=LIMIT, collective_id=0, has_side_effects=True
        ),
    )(x, w_query, w_out, agent_tokens, k7, k5, k3, values, stats)
    return out.reshape(rows, width, dim)


def solution(mesh):
    rows = P(("slide", "col"), None, None)
    return jax.shard_map(
        functools.partial(on_device, mesh.shape["col"]),
        mesh=mesh,
        in_specs=(rows, P(("slide", "col"), None)) + (P(),) * 8,
        out_specs=rows,
        check_vma=False,
    )
```

time: 211 us -> 54.7 us (0.26)
  the two profiles are of different devices: /device:TPU:0 before, /device:TPU:13 now
where the time goes in v1:
time: 54.7 us; the launch traced here: 54.5 us
  Pallas kernels  52.2 us (95%)
  local copies, waits for them, and re-layouts  2.26 us (4%)
    pallas_call x1, Pallas kernels, on_device(): pl.pallas_call(functools.partial(rest_kernel, n), out_shape=jax.ShapeDtyp...  44.8 us
    pallas_call x1, Pallas kernels, on_device(): pl.pallas_call(stats_kernel, out_shape=(jax.ShapeDtypeStruct((tokens, dim...  7.47 us
    unnamed x1, local copies, waits for them, and re-layouts  2.26 us

profile of v1, /device:TPU:13, one launch (start us, length us, event | category | flops | bytes accessed | tf_op | source)
XLA Modules:
  0.0 54.5 jit_solution(6529020385086519931)
XLA Ops:
  0.0 7.5 %shard_map.100 = (bf16[1024,512]{1,0:T(8,128)(2,1)}, f32[256,640]{1,0:T(8,128)}) custom-call(bf16[1024,512]{1,0:T(8,128)(2,1)} %bitcast.4, s32[8,128]{1,0:T(8,128)} %tissue_ref.1, bf16[512,512]{1,0:T(8,128)(2,1)} %wk_ref.1, bf16[512,512]{1,0:T(8,128)(2,1)} %wv_ref.1, bf16[256,512]{1,0:T(8,128)(2,1)} %ag_ref.3), custom_call_target="tpu_custom_call" | custom-call | tf_op jit(solution)/shard_map/pallas_call | solution.py:283
  7.5 44.8 %shard_map.101 = bf16[1024,512]{1,0:T(8,128)(2,1)} custom-call(bf16[1024,512]{1,0:T(8,128)(2,1)} %bitcast.5, bf16[512,512]{1,0:T(8,128)(2,1)} %wq_ref.1, bf16[512,512]{1,0:T(8,128)(2,1)} %wo_ref.1, bf16[256,512]{1,0:T(8,128)(2,1)} %ag_ref.3, f32[7,7,512]{2,1,0:T(8,128)} %k7_ref.1, f32[5,5,512]{2,1,0:T(8,128)} %k5_ref.1, f32[3,3,512]{2,1,0:T(4,128)} %k3_ref.1, ...), custom_call_target="tpu_custom_call" | custom-call | tf_op jit(solution)/shard_map/pallas_call | solution.py:304
  52.2 2.3 %copy.12 = bf16[8,128,512]{2,1,0:T(8,128)(2,1)} copy(bf16[8,128,512]{2,1,0:T(8,128)(2,1)} %bitcast.6) | data formatting | bytes 2097152

commit v2 on v1

--- a/solution.py
+++ b/solution.py
@@ -28,36 +28,44 @@
     return jnp.where(keep, pair, 0.0).astype(BF16)
 
 
-def stats_kernel(x_ref, tissue_ref, wk_ref, wv_ref, ag_ref, v_ref, st_ref, k_ref):
-    tokens, dim = x_ref.shape
+def project(x_ref, w_ref, out_ref):
+    width = out_ref.shape[1]
     chunk = 256
-    for c in range(0, tokens, chunk):
-        x = x_ref[c : c + chunk, :]
-        k_ref[c : c + chunk, :] = jnp.dot(x, wk_ref[...], preferred_element_type=F32).astype(BF16)
-        v_ref[c : c + chunk, :] = jnp.dot(x, wv_ref[...], preferred_element_type=F32).astype(BF16)
-    rows = tissue_ref.shape[0]
+    for c in range(0, x_ref.shape[0], chunk):
+        y = jnp.dot(x_ref[c : c + chunk, :], w_ref[...], preferred_element_type=F32).astype(BF16)
+        for r in range(chunk // width):
+            out_ref[c // width + r, :, :] = y[r * width : (r + 1) * width, :]
+
+
+def band_stats(tissue_ref, ag_ref, k_ref, v_ref, st_ref):
+    rows, width, dim = v_ref.shape
+    tokens = rows * width
+    n, own, _ = st_ref.shape
     tissue = jnp.concatenate([tissue_ref[r : r + 1, :] for r in range(rows)], axis=1) > 0
     agents = ag_ref.shape[0]
     lane = lax.broadcasted_iota(jnp.int32, (agents, LANES), 1)
     side = jnp.zeros((agents, LANES), F32)
+
+    def put(value, start):
+        for i in range(n):
+            st_ref[i, :, start : start + LANES] = value[i * own : (i + 1) * own, :]
+
     for pair in range(HEADS // 2):
         start = pair * LANES
+        keys = k_ref[:, :, start : start + LANES].reshape(tokens, LANES)
+        vals = v_ref[:, :, start : start + LANES].reshape(tokens, LANES)
         got = []
         for head in (2 * pair, 2 * pair + 1):
-            s = lax.dot_general(
-                head_agents(ag_ref, head), k_ref[:, start : start + LANES], NT, preferred_element_type=F32
-            )
+            s = lax.dot_general(head_agents(ag_ref, head), keys, NT, preferred_element_type=F32)
             s = jnp.where(tissue, s, NONE)
             top = jnp.max(s, axis=1, keepdims=True)
             e = jnp.exp(s - jnp.maximum(top, 0.1 * NONE))
             total = jnp.sum(e, axis=1, keepdims=True)
-            got.append(
-                jnp.dot(e.astype(BF16), v_ref[:, start : start + LANES], preferred_element_type=F32)
-            )
+            got.append(jnp.dot(e.astype(BF16), vals, preferred_element_type=F32))
             side = jnp.where(lane == head, top, side)
             side = jnp.where(lane == HEADS + head, total, side)
-        st_ref[:, start : start + LANES] = jnp.where(lane < LANES // 2, got[0], got[1])
-    st_ref[:, dim : dim + LANES] = side
+        put(jnp.where(lane < LANES // 2, got[0], got[1]), start)
+    put(side, dim)
 
 
 def token_side(x_ref, wq_ref, ag_ref, tw_ref):
@@ -100,16 +108,15 @@
             ext_ref[block, r + 3, 8 : width + 8, :] = v_ref[r, :, at].astype(F32)
 
 
-def fill_rim(rim_ref, ext_ref, first, there):
+def fill_rim(rim_ref, ext_ref, first):
     width = rim_ref.shape[1]
     for block in range(ext_ref.shape[0]):
         at = slice(block * LANES, block * LANES + LANES)
         for r in range(3):
-            rim = rim_ref[r, :, at].astype(F32)
-            ext_ref[block, first + r, 8 : width + 8, :] = jnp.where(there, rim, 0.0)
-
-
-def convolve(ext_ref, taps_ref, pos_ref):
+            ext_ref[block, first + r, 8 : width + 8, :] = rim_ref[r, :, at].astype(F32)
+
+
+def convolve(ext_ref, taps_ref, pos_ref, part, parts):
     blocks, ext_rows, _, _ = ext_ref.shape
     _, rows, width, _ = pos_ref.shape
     step = 16
@@ -128,10 +135,11 @@
             pos_ref[block, out, pl.ds(c, step), :] = sums[out]
         return carry
 
-    lax.fori_loop(0, blocks * (width // step), one, 0)
-
-
-def finish(av, tw_ref, pos_ref, wo_ref, out_ref):
+    steps = blocks * (width // step)
+    lax.fori_loop(part * steps // parts, (part + 1) * steps // parts, one, 0)
+
+
+def blend(av, tw_ref, pos_ref, out_ref):
     av_t = av.T
     blocks, _, width, _ = pos_ref.shape
     chunk = 256
@@ -153,8 +161,7 @@
             ],
             axis=0,
         )
-        blended = (attended + position).astype(BF16)
-        out_ref[c : c + chunk, :] = jnp.dot(blended, wo_ref[...], preferred_element_type=F32).astype(BF16)
+        out_ref[c : c + chunk, :] = (attended + position).astype(BF16)
 
 
 def combine(got_ref, dim):
@@ -202,18 +209,17 @@
         self.down = remote(v_ref.at[pl.ds(rows - 3, 3)], above_ref, s3.at[0], r3.at[0], lax.rem(me + 1, n))
         self.up = remote(v_ref.at[pl.ds(0, 3)], below_ref, s3.at[1], r3.at[1], lax.rem(me + n - 1, n))
 
-    def enter(self):
+    def greet(self):
         barrier = pltpu.get_barrier_semaphore()
         for p in self.to:
             pl.semaphore_signal(
                 barrier, inc=1, device_id={"col": p}, device_id_type=pl.DeviceIdType.MESH
             )
-        pl.semaphore_wait(barrier, self.n - 1)
-
-    def start(self):
-        for copy in self.scatter:
-            copy.start()
-
+
+    def met(self):
+        pl.semaphore_wait(pltpu.get_barrier_semaphore(), self.n - 1)
+
+    def send_rims(self):
         @pl.when(self.me < self.n - 1)
         def _():
             self.down.start()
@@ -222,6 +228,9 @@
         def _():
             self.up.start()
 
+    def send_stats(self):
+        for copy in self.scatter:
+            copy.start()
         self.got[self.me] = self.st[self.me]
 
     def reduce(self):
@@ -252,26 +261,32 @@
     return [dma((n - 1,)), dma((n - 1,)), dma((n - 1,)), dma((n - 1,)), dma((2,)), dma((2,))]
 
 
-def rest_kernel(
-    n, x_ref, wq_ref, wo_ref, ag_ref, k7_ref, k5_ref, k3_ref, v_ref, st_ref,
-    out_ref, av_ref, above_ref, below_ref, got_ref, tw_ref, taps_ref, ext_ref, pos_ref, *sems
+def whole_kernel(
+    n, x_ref, tissue_ref, wq_ref, wk_ref, wv_ref, ag_ref, k7_ref, k5_ref, k3_ref, out_ref,
+    v_ref, k_ref, st_ref, av_ref, above_ref, below_ref, got_ref, tw_ref, taps_ref, ext_ref, pos_ref, *sems
 ):
     work = Exchange(n, v_ref, st_ref, av_ref, above_ref, below_ref, got_ref, sems)
     above_ref[...] = jnp.zeros(above_ref.shape, BF16)
     below_ref[...] = jnp.zeros(below_ref.shape, BF16)
-    work.enter()
-    work.start()
+    work.greet()
+    project(x_ref, wv_ref, v_ref)
+    work.met()
+    work.send_rims()
+    project(x_ref, wk_ref, k_ref)
+    band_stats(tissue_ref, ag_ref, k_ref, v_ref, st_ref)
+    work.send_stats()
     spread_taps(k7_ref, k5_ref, k3_ref, taps_ref)
     fill_own(v_ref, ext_ref)
     token_side(x_ref, wq_ref, ag_ref, tw_ref)
+    work.rims()
+    fill_rim(above_ref, ext_ref, 0)
+    fill_rim(below_ref, ext_ref, ext_ref.shape[1] - 3)
+    convolve(ext_ref, taps_ref, pos_ref, 0, 2)
     work.reduce()
-    work.rims()
-    fill_rim(above_ref, ext_ref, 0, True)
-    fill_rim(below_ref, ext_ref, ext_ref.shape[1] - 3, True)
-    convolve(ext_ref, taps_ref, pos_ref)
+    convolve(ext_ref, taps_ref, pos_ref, 1, 2)
     work.end()
     av = jnp.concatenate([av_ref[i] for i in range(n)], axis=0)
-    finish(av, tw_ref, pos_ref, wo_ref, out_ref)
+    blend(av, tw_ref, pos_ref, out_ref)
 
 
 def on_device(n, patches, tissue, w_query, w_key, w_value, w_out, agent_tokens, k7, k5, k3):
@@ -280,45 +295,33 @@
     agents = agent_tokens.shape[0]
     own = agents // n
     x = patches.reshape(tokens, dim)
-    values, stats = pl.pallas_call(
-        stats_kernel,
-        out_shape=(
-            jax.ShapeDtypeStruct((tokens, dim), BF16),
-            jax.ShapeDtypeStruct((agents, dim + LANES), F32),
-        ),
-        in_specs=[VMEM] * 5,
-        out_specs=(VMEM, VMEM),
-        scratch_shapes=[pltpu.VMEM((tokens, dim), BF16)],
-        compiler_params=pltpu.CompilerParams(vmem_limit_bytes=LIMIT),
-    )(x, tissue, w_key, w_value, agent_tokens)
-    values = values.reshape(rows, width, dim)
-    stats = stats.reshape(n, own, dim + LANES)
     rim = (3, width, dim)
     blocks = dim // LANES
-    work = [
-        pltpu.VMEM((HEADS, agents, tokens), BF16),
-        pltpu.VMEM((blocks, 49, 8, LANES), F32),
-        pltpu.VMEM((blocks, rows + 6, width + 16, LANES), F32),
-        pltpu.VMEM((blocks, rows, width, LANES), F32),
-    ]
-    out = pl.pallas_call(
-        functools.partial(rest_kernel, n),
+    blended = pl.pallas_call(
+        functools.partial(whole_kernel, n),
         out_shape=jax.ShapeDtypeStruct((tokens, dim), BF16),
         in_specs=[VMEM] * 9,
         out_specs=VMEM,
         scratch_shapes=[
+            pltpu.VMEM((rows, width, dim), BF16),
+            pltpu.VMEM((rows, width, dim), BF16),
+            pltpu.VMEM((n, own, dim + LANES), F32),
             pltpu.VMEM((n, own, dim), BF16),
             pltpu.VMEM(rim, BF16),
             pltpu.VMEM(rim, BF16),
             pltpu.VMEM((n, own, dim + LANES), F32),
+            pltpu.VMEM((HEADS, agents, tokens), BF16),
+            pltpu.VMEM((blocks, 49, 8, LANES), F32),
+            pltpu.VMEM((blocks, rows + 6, width + 16, LANES), F32),
+            pltpu.VMEM((blocks, rows, width, LANES), F32),
         ]
-        + work
         + sem_shapes(n),
         compiler_params=pltpu.CompilerParams(
             vmem_limit_bytes=LIMIT, collective_id=0, has_side_effects=True
         ),
-    )(x, w_query, w_out, agent_tokens, k7, k5, k3, values, stats)
-    return out.reshape(rows, width, dim)
+    )(x, tissue, w_query, w_key, w_value, agent_tokens, k7, k5, k3)
+    mixed = jnp.dot(blended, w_out, preferred_element_type=F32).astype(BF16)
+    return mixed.reshape(rows, width, dim)
 
 
 def solution(mesh):

time: 54.7 us -> 39.5 us (0.72)
  the two profiles are of different devices: /device:TPU:13 before, /device:TPU:0 now
where the time goes in v2:
time: 39.5 us; the launch traced here: 39.4 us
  Pallas kernels  36.4 us (92%)
  matrix products  2.9 us (7%)
    pallas_call x1, Pallas kernels, on_device(): pl.pallas_call(functools.partial(whole_kernel, n), out_shape=jax.ShapeDty...  36.4 us
    dot_general x1, matrix products, on_device(): mixed = jnp.dot(blended, w_out, preferred_element_type=F32).astype(BF16)  2.9 us

profile of v2, /device:TPU:0, one launch (start us, length us, event | category | flops | bytes accessed | tf_op | source)
XLA Modules:
  0.0 39.4 jit_solution(5862364294084086354)
XLA Ops:
  0.0 0.0 copy-start
  0.0 36.4 %shard_map.100 = bf16[1024,512]{1,0:T(8,128)(2,1)} custom-call(bf16[1024,512]{1,0:T(8,128)(2,1)} %bitcast.4, s32[8,128]{1,0:T(8,128)} %tissue_ref.1, bf16[512,512]{1,0:T(8,128)(2,1)} %wq_ref.1, bf16[512,512]{1,0:T(8,128)(2,1)} %wk_ref.1, bf16[512,512]{1,0:T(8,128)(2,1)} %wv_ref.1, bf16[256,512]{1,0:T(8,128)(2,1)} %ag_ref.1, f32[7,7,512]{2,1,0:T(8,128)} %k7_ref.1, ...), custom_call_target="tpu_custom_call" | custom-call | tf_op jit(solution)/shard_map/pallas_call | solution.py:300
  36.4 0.0 copy-done
  36.5 2.9 %convolution_convert_fusion = bf16[1024,512]{1,0:T(8,128)(2,1)} fusion(bf16[1024,512]{1,0:T(8,128)(2,1)} %shard_map.100, bf16[512,512]{1,0:T(8,128)(2,1)S(1)} %copy-done), kind=kOutput, calls=%fused_computation | convolution fusion | flops 537395200 | bytes 2621440 | tf_op jit(solution)/shard_map/dot_general | solution.py:323
Async XLA Ops:
  0.0 36.4 %copy-start = (bf16[512,512]{1,0:T(8,128)(2,1)S(1)}, bf16[512,512]{1,0:T(8,128)(2,1)}, u32[]{:S(2)}) copy-start(bf16[512,512]{1,0:T(8,128)(2,1)} %param.15) | copy-start | bytes 1572868

commit v3 on v2

--- a/solution.py
+++ b/solution.py
@@ -28,6 +28,26 @@
     return jnp.where(keep, pair, 0.0).astype(BF16)
 
 
+def split_agents(ag_ref, heads_ref):
+    for head in range(HEADS):
+        heads_ref[head, :, :] = head_agents(ag_ref, head)
+
+
+def project_values(x_ref, w_ref, out_ref, ext_ref):
+    rows, width, dim = out_ref.shape
+    chunk = 256
+    for c in range(0, x_ref.shape[0], chunk):
+        y = jnp.dot(x_ref[c : c + chunk, :], w_ref[...], preferred_element_type=F32).astype(BF16)
+        wide = y.astype(F32)
+        for r in range(chunk // width):
+            row = c // width + r
+            out_ref[row, :, :] = y[r * width : (r + 1) * width, :]
+            for block in range(dim // LANES):
+                ext_ref[block, row + 3, 8 : width + 8, :] = wide[
+                    r * width : (r + 1) * width, block * LANES : (block + 1) * LANES
+                ]
+
+
 def project(x_ref, w_ref, out_ref):
     width = out_ref.shape[1]
     chunk = 256
@@ -37,12 +57,12 @@
             out_ref[c // width + r, :, :] = y[r * width : (r + 1) * width, :]
 
 
-def band_stats(tissue_ref, ag_ref, k_ref, v_ref, st_ref):
+def band_stats(tissue_ref, heads_ref, k_ref, v_ref, st_ref):
     rows, width, dim = v_ref.shape
     tokens = rows * width
     n, own, _ = st_ref.shape
     tissue = jnp.concatenate([tissue_ref[r : r + 1, :] for r in range(rows)], axis=1) > 0
-    agents = ag_ref.shape[0]
+    agents = heads_ref.shape[1]
     lane = lax.broadcasted_iota(jnp.int32, (agents, LANES), 1)
     side = jnp.zeros((agents, LANES), F32)
 
@@ -56,7 +76,7 @@
         vals = v_ref[:, :, start : start + LANES].reshape(tokens, LANES)
         got = []
         for head in (2 * pair, 2 * pair + 1):
-            s = lax.dot_general(head_agents(ag_ref, head), keys, NT, preferred_element_type=F32)
+            s = lax.dot_general(heads_ref[head], keys, NT, preferred_element_type=F32)
             s = jnp.where(tissue, s, NONE)
             top = jnp.max(s, axis=1, keepdims=True)
             e = jnp.exp(s - jnp.maximum(top, 0.1 * NONE))
@@ -68,7 +88,7 @@
     put(side, dim)
 
 
-def token_side(x_ref, wq_ref, ag_ref, tw_ref):
+def token_side(x_ref, wq_ref, heads_ref, tw_ref):
     tokens = x_ref.shape[0]
     chunk = 256
     for c in range(0, tokens, chunk):
@@ -76,7 +96,7 @@
         for head in range(HEADS):
             start = head // 2 * LANES
             s = lax.dot_general(
-                head_agents(ag_ref, head), q[:, start : start + LANES], NT, preferred_element_type=F32
+                heads_ref[head], q[:, start : start + LANES], NT, preferred_element_type=F32
             )
             e = jnp.exp(s - jnp.max(s, axis=0, keepdims=True))
             share = 1.0 / jnp.sum(e, axis=0, keepdims=True)
@@ -96,16 +116,12 @@
                 taps_ref[block, p * 7 + q, :, :] = jnp.broadcast_to(tap, (8, LANES))
 
 
-def fill_own(v_ref, ext_ref):
-    blocks, ext_rows, _, _ = ext_ref.shape
-    width = v_ref.shape[1]
+def fill_sides(ext_ref):
+    blocks, ext_rows, padded, _ = ext_ref.shape
     for block in range(blocks):
-        at = slice(block * LANES, block * LANES + LANES)
         for r in range(ext_rows):
             ext_ref[block, r, 0:8, :] = jnp.zeros((8, LANES), F32)
-            ext_ref[block, r, width + 8 : width + 16, :] = jnp.zeros((8, LANES), F32)
-        for r in range(ext_rows - 6):
-            ext_ref[block, r + 3, 8 : width + 8, :] = v_ref[r, :, at].astype(F32)
+            ext_ref[block, r, padded - 8 : padded, :] = jnp.zeros((8, LANES), F32)
 
 
 def fill_rim(rim_ref, ext_ref, first):
@@ -119,24 +135,23 @@
 def convolve(ext_ref, taps_ref, pos_ref, part, parts):
     blocks, ext_rows, _, _ = ext_ref.shape
     _, rows, width, _ = pos_ref.shape
-    step = 16
-
-    def one(i, carry):
-        block = i // (width // step)
-        c = pl.multiple_of(i % (width // step) * step, step)
-        sums = [jnp.zeros((step, LANES), F32) for _ in range(rows)]
-        for q in range(7):
-            taps = [jnp.concatenate([taps_ref[block, p * 7 + q]] * (step // 8), axis=0) for p in range(7)]
-            for r in range(ext_rows):
-                x = ext_ref[block, r, pl.ds(c + (5 + q), step), :]
-                for out in range(max(r - 6, 0), min(r + 1, rows)):
-                    sums[out] = sums[out] + x * taps[r - out]
-        for out in range(rows):
-            pos_ref[block, out, pl.ds(c, step), :] = sums[out]
+    step = 8
+
+    def one(block, carry):
+        for c in range(0, width, step):
+            sums = [None] * rows
+            for q in range(7):
+                taps = [taps_ref[block, p * 7 + q] for p in range(7)]
+                for r in range(ext_rows):
+                    x = ext_ref[block, r, c + 5 + q : c + 5 + q + step, :]
+                    for out in range(max(r - 6, 0), min(r + 1, rows)):
+                        term = x * taps[r - out]
+                        sums[out] = term if sums[out] is None else sums[out] + term
+            for out in range(rows):
+                pos_ref[block, out, c : c + step, :] = sums[out]
         return carry
 
-    steps = blocks * (width // step)
-    lax.fori_loop(part * steps // parts, (part + 1) * steps // parts, one, 0)
+    lax.fori_loop(part * blocks // parts, (part + 1) * blocks // parts, one, 0)
 
 
 def blend(av, tw_ref, pos_ref, out_ref):
@@ -261,23 +276,36 @@
     return [dma((n - 1,)), dma((n - 1,)), dma((n - 1,)), dma((n - 1,)), dma((2,)), dma((2,))]
 
 
-def whole_kernel(
-    n, x_ref, tissue_ref, wq_ref, wk_ref, wv_ref, ag_ref, k7_ref, k5_ref, k3_ref, out_ref,
-    v_ref, k_ref, st_ref, av_ref, above_ref, below_ref, got_ref, tw_ref, taps_ref, ext_ref, pos_ref, *sems
-):
+def whole_kernel(n, *refs):
+    sources, out_ref = refs[:9], refs[9]
+    held, load_sem = refs[10:19], refs[19]
+    x_ref, tissue_ref, wq_ref, wk_ref, wv_ref, ag_ref, k7_ref, k5_ref, k3_ref = held
+    (v_ref, k_ref, st_ref, av_ref, above_ref, below_ref, got_ref, tw_ref, taps_ref, ext_ref, pos_ref,
+     heads_ref, *sems) = refs[20:]
+    loads = [pltpu.make_async_copy(sources[i], held[i], load_sem.at[i]) for i in range(9)]
+    for i in (0, 4, 3, 5, 1, 6, 7, 8, 2):
+        loads[i].start()
     work = Exchange(n, v_ref, st_ref, av_ref, above_ref, below_ref, got_ref, sems)
     above_ref[...] = jnp.zeros(above_ref.shape, BF16)
     below_ref[...] = jnp.zeros(below_ref.shape, BF16)
     work.greet()
-    project(x_ref, wv_ref, v_ref)
+    fill_sides(ext_ref)
+    loads[0].wait()
+    loads[4].wait()
+    project_values(x_ref, wv_ref, v_ref, ext_ref)
+    loads[5].wait()
+    split_agents(ag_ref, heads_ref)
     work.met()
     work.send_rims()
+    loads[3].wait()
+    loads[1].wait()
     project(x_ref, wk_ref, k_ref)
-    band_stats(tissue_ref, ag_ref, k_ref, v_ref, st_ref)
+    band_stats(tissue_ref, heads_ref, k_ref, v_ref, st_ref)
     work.send_stats()
+    for i in (6, 7, 8, 2):
+        loads[i].wait()
     spread_taps(k7_ref, k5_ref, k3_ref, taps_ref)
-    fill_own(v_ref, ext_ref)
-    token_side(x_ref, wq_ref, ag_ref, tw_ref)
+    token_side(x_ref, wq_ref, heads_ref, tw_ref)
     work.rims()
     fill_rim(above_ref, ext_ref, 0)
     fill_rim(below_ref, ext_ref, ext_ref.shape[1] - 3)
@@ -297,12 +325,15 @@
     x = patches.reshape(tokens, dim)
     rim = (3, width, dim)
     blocks = dim // LANES
+    given = (x, tissue, w_query, w_key, w_value, agent_tokens, k7, k5, k3)
     blended = pl.pallas_call(
         functools.partial(whole_kernel, n),
         out_shape=jax.ShapeDtypeStruct((tokens, dim), BF16),
-        in_specs=[VMEM] * 9,
+        in_specs=[pl.BlockSpec(memory_space=pltpu.HBM)] * len(given),
         out_specs=VMEM,
-        scratch_shapes=[
+        scratch_shapes=[pltpu.VMEM(a.shape, a.dtype) for a in given]
+        + [
+            pltpu.SemaphoreType.DMA((len(given),)),
             pltpu.VMEM((rows, width, dim), BF16),
             pltpu.VMEM((rows, width, dim), BF16),
             pltpu.VMEM((n, own, dim + LANES), F32),
@@ -314,12 +345,13 @@
             pltpu.VMEM((blocks, 49, 8, LANES), F32),
             pltpu.VMEM((blocks, rows + 6, width + 16, LANES), F32),
             pltpu.VMEM((blocks, rows, width, LANES), F32),
+            pltpu.VMEM((HEADS, agents, LANES), BF16),
         ]
         + sem_shapes(n),
         compiler_params=pltpu.CompilerParams(
             vmem_limit_bytes=LIMIT, collective_id=0, has_side_effects=True
         ),
-    )(x, tissue, w_query, w_key, w_value, agent_tokens, k7, k5, k3)
+    )(*given)
     mixed = jnp.dot(blended, w_out, preferred_element_type=F32).astype(BF16)
     return mixed.reshape(rows, width, dim)
 

time: 39.5 us -> 37.7 us (0.954)
  Pallas kernels: 36.4 us -> 34.7 us
    pallas_call x1, Pallas kernels: 36.4 us -> 34.7 us  [on_device(): pl.pallas_call(functools.partial(whole_kernel, n), out_shape=jax.ShapeDty...]
where the time goes in v3:
time: 37.7 us; the launch traced here: 37.6 us
  Pallas kernels  34.7 us (92%)
  matrix products  2.9 us (8%)
    pallas_call x1, Pallas kernels, on_device(): pl.pallas_call(functools.partial(whole_kernel, n), out_shape=jax.ShapeDty...  34.7 us
    dot_general x1, matrix products, on_device(): mixed = jnp.dot(blended, w_out, preferred_element_type=F32).astype(BF16)  2.9 us

profile of v3, /device:TPU:0, one launch (start us, length us, event | category | flops | bytes accessed | tf_op | source)
XLA Modules:
  0.0 37.6 jit_solution(12893882266934744012)
XLA Ops:
  0.0 0.0 copy-start
  0.0 34.7 %shard_map.100 = bf16[1024,512]{1,0:T(8,128)(2,1)} custom-call(bf16[1024,512]{1,0:T(8,128)(2,1)} %bitcast.4, s32[8,128]{1,0:T(8,128)} %refs_1_.1, bf16[512,512]{1,0:T(8,128)(2,1)} %refs_2_.1, bf16[512,512]{1,0:T(8,128)(2,1)} %refs_3_.1, bf16[512,512]{1,0:T(8,128)(2,1)} %refs_4_.1, bf16[256,512]{1,0:T(8,128)(2,1)} %refs_5_.1, f32[7,7,512]{2,1,0:T(8,128)} %refs_6_.1, ...), custom_call_target="tpu_custom_call" | custom-call | tf_op jit(solution)/shard_map/pallas_call | solution.py:329
  34.7 0.0 copy-done
  34.7 2.9 %convolution_convert_fusion = bf16[1024,512]{1,0:T(8,128)(2,1)} fusion(bf16[1024,512]{1,0:T(8,128)(2,1)} %shard_map.100, bf16[512,512]{1,0:T(8,128)(2,1)S(1)} %copy-done), kind=kOutput, calls=%fused_computation | convolution fusion | flops 537395200 | bytes 2621440 | tf_op jit(solution)/shard_map/dot_general | solution.py:355
Async XLA Ops:
  0.0 34.7 %copy-start = (bf16[512,512]{1,0:T(8,128)(2,1)S(1)}, bf16[512,512]{1,0:T(8,128)(2,1)}, u32[]{:S(2)}) copy-start(bf16[512,512]{1,0:T(8,128)(2,1)} %param.15) | copy-start | bytes 1572868
